TPU v7x, 32 devices: a whole 2x2x4 slice. The times are simulated.
32 devices in a mesh: az: 4 (over z), rad: 2 (over x), ax: 4 (over y, core).
Axes of the slice: x: 2, y: 2, z: 4, core: 2. Of those that a mesh axis runs over, the one named last changes fastest.
Arguments:
- cycle: float32 [4, 5, 512, 4096], P(None, None, ('rad', 'ax'), 'az'), may hold values from -6 to 6
- field: float32 [5, 64, 8, 4096], P(None, 'rad', 'ax', 'az'), may hold values from -6 to 6
- shift: int32 [1], replicated, may hold values from 0 to 4095
- owner: int32 [64, 8], P('rad', 'ax'), may hold values 0 or 1
Outputs:
- field_next: float32 [5, 64, 8, 4096], P(None, 'rad', 'ax', 'az')
- shifted_cycle: float32 [4, 5, 512, 4096], P(None, None, ('rad', 'ax'), 'az')
All inputs are finite; a program needn't handle non-finite values. No bound on the sum of `owner` on one device may be relied on, other than what follows from the above.
Results may differ from a plain program's by a relative error of at most 0.00007.
Values sent between devices are 32-bit elements; how exact they have to be, the bound alone decides.
A program may use at most 192 MiB of HBM per device.

v0:
```python
import math
import jax
import jax.numpy as jnp
from jax import lax
from jax.sharding import PartitionSpec as P

KR = 8
LAYER_WEIGHTS = (0.4, 0.3, 0.2, 0.1)
AXIAL_SPEEDS = (0.35, 0.2, 0.3, 0.25, 0.4)
DIFFUSION = 0.15
SWIRL_SPEED = 0.1


def padded(array, sides, width):
    for axis, dim in sides:
        devices, length = (lax.axis_size(axis), array.shape[dim])
        up = [(i, (i + 1) % devices) for i in range(devices - 1)]
        down = [(j, i) for i, j in up]
        last = lax.slice_in_dim(array, length - width, length, axis=dim)
        leading = lax.slice_in_dim(array, 0, width, axis=dim)
        before = lax.ppermute(last, axis, up)
        after = lax.ppermute(leading, axis, down)
        array = jnp.concatenate([before, array, after], axis=dim)
    return array


def turn_table(first, second, modulus):
    product = jnp.remainder(first[:, None] * second[None, :], modulus).astype(jnp.float32)
    angle = product * (2.0 * math.pi / modulus)
    return (jnp.cos(angle), jnp.sin(angle))


def spectral_shift(rows, shift_value):
    count, length = rows.shape
    half_bits = (length.bit_length() - 1) // 2
    outer = 2**half_bits
    inner = length // outer
    hp = lax.Precision.HIGHEST
    outer_index = jnp.arange(outer, dtype=jnp.int32)
    inner_index = jnp.arange(inner, dtype=jnp.int32)
    cos_outer, sin_outer = turn_table(outer_index, outer_index, outer)
    cos_inner, sin_inner = turn_table(inner_index, inner_index, inner)
    cos_twist, sin_twist = turn_table(outer_index, inner_index, length)
    grid = rows.reshape(count, outer, inner)
    section_re = jnp.einsum("bpq,pk->bkq", grid, cos_outer, precision=hp)
    section_im = -jnp.einsum("bpq,pk->bkq", grid, sin_outer, precision=hp)
    twist_re = section_re * cos_twist + section_im * sin_twist
    twist_im = section_im * cos_twist - section_re * sin_twist
    spec_re = jnp.einsum("bkq,qm->bkm", twist_re, cos_inner, precision=hp) + jnp.einsum(
        "bkq,qm->bkm", twist_im, sin_inner, precision=hp
    )
    spec_im = jnp.einsum("bkq,qm->bkm", twist_im, cos_inner, precision=hp) - jnp.einsum(
        "bkq,qm->bkm", twist_re, sin_inner, precision=hp
    )
    wave = outer_index[:, None] + outer * inner_index[None, :]
    folded = jnp.minimum(wave, length - wave)
    filt = (3 * folded < length).astype(jnp.float32)
    phase = jnp.remainder(wave * shift_value, length).astype(jnp.float32) * (2.0 * math.pi / length)
    gain_re = filt * jnp.cos(phase)
    gain_im = -filt * jnp.sin(phase)
    mixed_re = spec_re * gain_re - spec_im * gain_im
    mixed_im = spec_re * gain_im + spec_im * gain_re
    back_re = jnp.einsum("bkm,qm->bkq", mixed_re, cos_inner, precision=hp) - jnp.einsum(
        "bkm,qm->bkq", mixed_im, sin_inner, precision=hp
    )
    back_im = jnp.einsum("bkm,qm->bkq", mixed_im, cos_inner, precision=hp) + jnp.einsum(
        "bkm,qm->bkq", mixed_re, sin_inner, precision=hp
    )
    turn_re = back_re * cos_twist - back_im * sin_twist
    turn_im = back_im * cos_twist + back_re * sin_twist
    result = jnp.einsum("bkq,pk->bpq", turn_re, cos_outer, precision=hp) - jnp.einsum(
        "bkq,pk->bpq", turn_im, sin_outer, precision=hp
    )
    return (result / length).reshape(count, length)


def on_device(cycle, field, shift, owner):
    layers, variables, radial, sector = cycle.shape
    stacked = cycle.reshape(layers * variables, radial, sector)
    shift_value = shift[0]
    piece = lax.all_to_all(stacked, "az", split_axis=1, concat_axis=2, tiled=True)
    moved = spectral_shift(piece.reshape(-1, piece.shape[2]), shift_value).reshape(piece.shape)
    shifted_flat = lax.all_to_all(moved, "az", split_axis=2, concat_axis=1, tiled=True)
    shifted_cycle = shifted_flat.reshape(layers, variables, radial, sector)
    weights = jnp.array(LAYER_WEIGHTS, jnp.float32)
    depth, count, rows, width = shifted_cycle.shape
    grouped = shifted_cycle.reshape(depth, count, rows // KR, KR, width)
    ghost = lax.all_gather(
        jnp.einsum("l,lvrkt->vrt", weights, grouped, precision=lax.Precision.HIGHEST) / KR,
        "ax",
        axis=1,
        tiled=True,
    )
    mask = owner.astype(jnp.float32)[None, :, :, None]
    speeds = jnp.array(AXIAL_SPEEDS, jnp.float32)[:, None, None, None]
    at_inlet = lax.axis_index("ax") == 0

    def rates(state):
        radial_pad = padded(state, (("rad", 1),), 1)
        axial_pad = padded(state, (("ax", 2),), 1)
        lower = jnp.where(at_inlet, ghost, axial_pad[:, :, 0])
        outward = radial_pad[:, 2:]
        inward = radial_pad[:, :-2]
        above = axial_pad[:, :, 2:]
        below = jnp.concatenate([lower[:, :, None], axial_pad[:, :, 1:-2]], axis=2)
        return mask * (
            DIFFUSION * (outward + inward + above + below - 4.0 * state)
            - 0.5 * speeds * (above - below)
            - 0.5 * SWIRL_SPEED * (outward - inward)
        )

    first = rates(field)
    second = rates(field + 0.5 * first)
    third = rates(field + 0.5 * second)
    fourth = rates(field + third)
    field_next = field + (first + 2.0 * second + 2.0 * third + fourth) / 6.0
    return (field_next, shifted_cycle)


def solution(mesh):
    in_specs = (P(None, None, ("rad", "ax"), "az"), P(None, "rad", "ax", "az"), P(), P("rad", "ax"))
    out_specs = (P(None, "rad", "ax", "az"), P(None, None, ("rad", "ax"), "az"))
    return jax.shard_map(
        on_device, mesh=mesh, in_specs=in_specs, out_specs=out_specs, check_vma=False
    )
```

profile of v0, /device:TPU:1, one launch (start us, length us, event | category | flops | bytes accessed | tf_op | source)
XLA Modules:
  0.0 716.4 jit_solution(15796967327889109579)
XLA Ops:
  0.6 8.2 %copy.187 = f32[20,64,1024]{2,0,1:T(8,128)} copy(f32[20,64,1024]{2,1,0:T(8,128)} %bitcast.97) | data formatting | bytes 10485760 | tf_op jit(solution)/shard_map/reshape | solution.py:79
  8.8 5.6 all-to-all-start
  15.6 137.3 %all-to-all-done = f32[20,64,1024]{2,0,1:T(8,128)} async-done(((f32[20,64,1024]{2,0,1:T(8,128)}), f32[20,64,1024]{2,0,1:T(8,128)}, u32[]{:S(2)}, u32[]{:S(2)}) %all-to-all-start) | async-done | bytes 5242912 | tf_op jit(solution)/shard_map/all_to_all | solution.py:81
  152.9 8.5 %copy.189 = f32[20,16,4,1024]{3,2,1,0:T(4,128)} copy(f32[20,16,4,1024]{3,0,1,2:T(8,128)} %bitcast.5) | data formatting | bytes 10485760 | tf_op jit(solution)/shard_map/all_to_all | solution.py:81
  161.4 9.6 %reshape_reshape.9 = f32[320,64,64]{2,1,0:T(8,128)} reshape(f32[20,16,4,1024]{3,2,1,0:T(4,128)} %copy.189) | data formatting | bytes 10485760 | tf_op jit(solution)/shard_map/reshape;reshape | solution.py:44
  171.1 11.8 %copy.191 = f32[320,64,64]{0,1,2:T(8,128)} copy(f32[320,64,64]{2,1,0:T(8,128)} %reshape_reshape.9) | data formatting | bytes 10485760 | tf_op jit(solution)/shard_map/reshape;reshape | solution.py:44
  182.9 8.7 %fusion.44 = f32[64,320,64]{1,0,2:T(8,128)S(1)} fusion(f32[320,64,64]{0,1,2:T(8,128)} %copy.191), kind=kOutput, calls=%fused_computation.85 | convolution fusion | flops 1006690304 | bytes 10485760 | tf_op jit(solution)/shard_map/bpq,pk->bkq/dot_general | solution.py:46
  191.6 7.6 %add_bitcast_fusion = (f32[320,64,64]{0,1,2:T(8,128)S(1)}, f32[320,64,64]{0,1,2:T(8,128)S(1)}) fusion(f32[64,320,64]{1,0,2:T(8,128)S(1)} %fusion.44, f32[64,64]{0,1:T(8,128)S(1)} %copy.195, f32[64,64]{0,1:T(8,128)S(1)} %copy.192, f32[320,64,64]{0,1,2:T(8,128)S(1)} %copy-done.2), kind=kOutput, calls=%fused_computation.10 | convolution fusion | flops 1015865344 | bytes 21004288 | tf_op jit(solution)/shard_map/bpq,pk->bkq/dot_general | solution.py:45
  199.2 14.0 %fusion.10 = f32[320,64,64]{0,2,1:T(8,128)} fusion(f32[320,64,64]{0,1,2:T(8,128)S(1)} %get-tuple-element.16), kind=kOutput, calls=%fused_computation.17 | convolution fusion | flops 1006690304 | bytes 10485760 | tf_op jit(solution)/shard_map/bkq,qm->bkm/dot_general | solution.py:49
  213.2 13.2 %fusion.8 = f32[320,64,64]{0,2,1:T(8,128)} fusion(f32[320,64,64]{0,1,2:T(8,128)S(1)} %get-tuple-element.16), kind=kOutput, calls=%fused_computation.15 | convolution fusion | flops 1006690304 | bytes 10485760 | tf_op jit(solution)/shard_map/bkq,qm->bkm/dot_general | solution.py:52
  226.4 13.3 %fusion.6 = f32[320,64,64]{0,2,1:T(8,128)} fusion(f32[320,64,64]{0,1,2:T(8,128)S(1)} %get-tuple-element.17), kind=kOutput, calls=%fused_computation.13 | convolution fusion | flops 1006690304 | bytes 10485760 | tf_op jit(solution)/shard_map/bkq,qm->bkm/dot_general | solution.py:49
  239.7 19.1 %multiply_subtract_fusion.1 = (f32[320,64,64]{0,2,1:T(8,128)}, f32[320,64,64]{0,2,1:T(8,128)S(1)}) fusion(f32[64,64]{1,0:T(8,128)S(1)} %get-tuple-element.35, f32[64,64]{1,0:T(8,128)S(1)} %get-tuple-element.34, f32[320,64,64]{0,2,1:T(8,128)} %fusion.8, f32[320,64,64]{0,2,1:T(8,128)} %fusion.10, f32[320,64,64]{0,2,1:T(8,128)} %fusion.6, ...), kind=kOutput, calls=%fused_computation.8 | convolution fusion | flops 1017176064 | bytes 31490048 | tf_op jit(solution)/shard_map/bkq,qm->bkm/dot_general | solution.py:52
  258.9 10.3 %fusion.38 = f32[320,64,64]{0,2,1:T(8,128)} fusion(f32[320,64,64]{0,2,1:T(8,128)} %get-tuple-element.14), kind=kOutput, calls=%fused_computation.79 | convolution fusion | flops 1006690304 | bytes 10485760 | tf_op jit(solution)/shard_map/bkm,qm->bkq/dot_general | solution.py:66
  269.2 7.8 %fusion.53 = f32[320,64,64]{0,2,1:T(8,128)} fusion(f32[320,64,64]{0,2,1:T(8,128)S(1)} %copy-done), kind=kOutput, calls=%fused_computation.94 | convolution fusion | flops 1006690304 | bytes 10485760 | tf_op jit(solution)/shard_map/bkm,qm->bkq/dot_general | solution.py:63
  277.0 7.9 %fusion.40 = f32[320,64,64]{0,2,1:T(8,128)} fusion(f32[320,64,64]{0,2,1:T(8,128)S(1)} %get-tuple-element.15), kind=kOutput, calls=%fused_computation.81 | convolution fusion | flops 1006690304 | bytes 10485760 | tf_op jit(solution)/shard_map/bkm,qm->bkq/dot_general | solution.py:63
  284.9 15.2 %multiply_subtract_fusion = (f32[320,64,64]{0,2,1:T(8,128)}, f32[320,64,64]{0,2,1:T(8,128)}) fusion(f32[64,64]{1,0:T(8,128)S(1)} %get-tuple-element.36, f32[64,64]{1,0:T(8,128)S(1)} %get-tuple-element.37, f32[320,64,64]{0,2,1:T(8,128)} %fusion.38, f32[320,64,64]{0,2,1:T(8,128)} %fusion.53, f32[320,64,64]{0,2,1:T(8,128)} %fusion.40, ...), kind=kOutput, calls=%fused_computation.6 | convolution fusion | flops 1017176064 | bytes 31490048 | tf_op jit(solution)/shard_map/bkm,qm->bkq/dot_general | solution.py:66
  300.1 12.4 %fusion = f32[64,320,64]{1,0,2:T(8,128)S(1)} fusion(f32[320,64,64]{0,2,1:T(8,128)} %get-tuple-element.13), kind=kOutput, calls=%fused_computation | convolution fusion | flops 1006690304 | bytes 10485760 | tf_op jit(solution)/shard_map/bkq,pk->bpq/dot_general | solution.py:71
  312.5 11.2 %multiply_bitcast_fusion = f32[320,64,64]{0,1,2:T(8,128)} fusion(f32[64,320,64]{1,0,2:T(8,128)S(1)} %fusion, f32[320,64,64]{0,2,1:T(8,128)S(1)} %copy-done.3), kind=kOutput, calls=%fused_computation.4 | convolution fusion | flops 1009311744 | bytes 15728640 | tf_op jit(solution)/shard_map/bkq,pk->bpq/dot_general | solution.py:71
  323.7 12.6 %copy.206 = f32[320,64,64]{2,1,0:T(8,128)} copy(f32[320,64,64]{0,1,2:T(8,128)} %multiply_bitcast_fusion) | data formatting | bytes 10485760 | tf_op jit(solution)/shard_map/div | solution.py:74
  336.2 9.7 %reshape_reshape.10 = f32[20,16,4096]{2,1,0:T(8,128)} reshape(f32[320,64,64]{2,1,0:T(8,128)} %copy.206) | data formatting | bytes 10485760 | tf_op jit(solution)/shard_map/reshape;reshape | solution.py:82
  346.0 18.7 %copy.207 = f32[20,16,4096]{0,1,2:T(8,128)} copy(f32[20,16,4096]{2,1,0:T(8,128)} %reshape_reshape.10) | data formatting | bytes 10485760 | tf_op jit(solution)/shard_map/reshape;reshape | solution.py:82
  364.7 56.1 %reshape.131 = f32[4,1,327680]{2,1,0:T(1,128)} reshape(f32[4096,16,20]{2,1,0:T(8,128)} %bitcast.92) | data formatting | bytes 10485760
  420.9 5.2 all-to-all-start.1
  427.5 4.3 collective-permute-start.3
  439.1 102.1 %all-to-all-done.1 = f32[4,1,327680]{2,1,0:T(1,128)} async-done(((f32[4,1,327680]{2,1,0:T(1,128)}), f32[4,1,327680]{2,1,0:T(1,128)}, u32[]{:S(2)}, u32[]{:S(2)}) %all-to-all-start.1) | async-done | bytes 5242912 | tf_op jit(solution)/shard_map/all_to_all | solution.py:83
  541.8 18.3 %reduce = f32[4,327680]{1,0:T(4,128)} reduce(f32[4,1,327680]{2,1,0:T(1,128)} %all-to-all-done.1, f32[]{:T(128)} %broadcast.363), dimensions={1}, to_apply=%all_to_all.25.reduce_sub_computation | reduce | bytes 10485764 | tf_op jit(solution)/shard_map/all_to_all | solution.py:83
  560.1 52.9 %reshape.132 = f32[4096,16,20]{2,1,0:T(8,128)} reshape(f32[4,327680]{1,0:T(4,128)} %reduce) | data formatting | bytes 10485760
  613.0 22.4 %copy.234 = f32[20,16,4,1024]{3,2,1,0:T(4,128)} copy(f32[20,16,4,1024]{0,1,3,2:T(8,128)} %bitcast.93) | data formatting | bytes 10485760 | tf_op jit(solution)/shard_map/all_to_all | solution.py:83
  635.4 9.2 %copy.209 = f32[20,4,16,1024]{3,2,1,0:T(8,128)} copy(f32[20,4,16,1024]{3,1,2,0:T(4,128)} %bitcast.94) | data formatting | bytes 10485760 | tf_op jit(solution)/shard_map/all_to_all | solution.py:83
  644.6 4.6 reduce_sum.9
  651.9 9.0 %all_gather.3 = f32[5,32,1024]{2,1,0:T(8,128)S(1)} all-gather(f32[5,8,1024]{2,1,0:T(8,128)S(1)} %bitcast_multiply_fusion), channel_id=1, replica_groups=mesh['az'=4,'rad'=2,'ax'=4] {'ax'}, dimensions={1}, use_global_device_ids=true | all-gather | bytes 819200 | tf_op jit(solution)/shard_map/all_gather | solution.py:88
  708.6 5.5 multiply_add_fusion.2
  (75 shorter events, 62.1 us)
Async XLA Ops:
  8.8 144.1 %all-to-all-start = ((f32[20,64,1024]{2,0,1:T(8,128)}), f32[20,64,1024]{2,0,1:T(8,128)}, u32[]{:S(2)}, u32[]{:S(2)}) async-start(f32[20,64,1024]{2,0,1:T(8,128)} %copy.187), calls=%async_computation | async-start | bytes 12582912 | tf_op jit(solution)/shard_map/all_to_all | solution.py:81
  182.9 8.7 %copy-start.2 = (f32[320,64,64]{0,1,2:T(8,128)S(1)}, f32[320,64,64]{0,1,2:T(8,128)}, u32[]{:S(2)}) copy-start(f32[320,64,64]{0,1,2:T(8,128)} %copy.191) | copy-start | bytes 15728644
  199.2 27.2 %copy-start.1 = (f32[320,64,64]{0,1,2:T(8,128)}, f32[320,64,64]{0,1,2:T(8,128)S(1)}, u32[]{:S(2)}) copy-start(f32[320,64,64]{0,1,2:T(8,128)S(1)} %get-tuple-element.17) | copy-start | bytes 15728644
  258.9 10.3 %copy-start = (f32[320,64,64]{0,2,1:T(8,128)S(1)}, f32[320,64,64]{0,2,1:T(8,128)}, u32[]{:S(2)}) copy-start(f32[320,64,64]{0,2,1:T(8,128)} %get-tuple-element.14) | copy-start | bytes 15728644
  300.1 12.4 %copy-start.3 = (f32[320,64,64]{0,2,1:T(8,128)S(1)}, f32[320,64,64]{0,2,1:T(8,128)}, u32[]{:S(2)}) copy-start(f32[320,64,64]{0,2,1:T(8,128)} %get-tuple-element.12) | copy-start | bytes 15728644
  420.9 5.2 copy-start.4
  420.9 120.3 %all-to-all-start.1 = ((f32[4,1,327680]{2,1,0:T(1,128)}), f32[4,1,327680]{2,1,0:T(1,128)}, u32[]{:S(2)}, u32[]{:S(2)}) async-start(f32[4,1,327680]{2,1,0:T(1,128)} %reshape.131), calls=%async_computation.1 | async-start | bytes 10485760 | tf_op jit(solution)/shard_map/all_to_all | solution.py:83
  426.5 12.6 %copy-start.6 = (s32[32,2]{0,1:T(2,128)S(1)}, s32[32,2]{0,1:T(2,128)}, u32[]{:S(2)}) copy-start(s32[32,2]{0,1:T(2,128)} %param.9) | copy-start | bytes 772
  427.5 233.4 %collective-permute-start.3 = (f32[5,32,1,1024]{3,1,0,2:T(8,128)}, f32[5,32,1,1024]{3,1,0,2:T(8,128)}, u32[]{:S(2)}, u32[]{:S(2)}) collective-permute-start(f32[5,32,1,1024]{3,1,0,2:T(8,128)} %get-tuple-element.30), channel_id=1, source_target_pairs={{0,1},{1,2},{2,3},{4,5},{5,6},{6,7},{8,9},{9,10},{10,11},{12,13},{... | collective-permute-start | bytes 1966088 | tf_op jit(solution)/shard_map/ppermute | solution.py:21
  431.8 230.3 %collective-permute-start.2 = (f32[5,32,1,1024]{3,1,0,2:T(8,128)S(1)}, f32[5,32,1,1024]{3,1,0,2:T(8,128)}, u32[]{:S(2)}, u32[]{:S(2)}) collective-permute-start(f32[5,32,1,1024]{3,1,0,2:T(8,128)S(1)} %get-tuple-element.31), channel_id=1, source_target_pairs={{1,0},{2,1},{3,2},{5,4},{6,5},{7,6},{9,8},{10,9},{11,10},{13,12},{... | collective-permute-start | bytes 1966088 | tf_op jit(solution)/shard_map/ppermute | solution.py:22
  433.8 228.3 %collective-permute-start = (f32[5,1,2,1024]{3,1,0,2:T(1,128)S(1)}, f32[5,1,2,1024]{3,1,0,2:T(1,128)S(1)}, u32[]{:S(2)}, u32[]{:S(2)}) collective-permute-start(f32[5,1,2,1024]{3,1,0,2:T(1,128)S(1)} %copy.181), channel_id=1, source_target_pairs={{4,0},{5,1},{6,2},{7,3},{12,8},{13,9},{14,10},{15,11},{20,16},{21,... | collective-permute-start | bytes 122888 | tf_op jit(solution)/shard_map/ppermute | solution.py:22
  435.1 227.0 %collective-permute-start.1 = (f32[5,1,2,1024]{3,1,0,2:T(1,128)S(1)}, f32[5,1,2,1024]{3,1,0,2:T(1,128)S(1)}, u32[]{:S(2)}, u32[]{:S(2)}) collective-permute-start(f32[5,1,2,1024]{3,1,0,2:T(1,128)S(1)} %copy.183), channel_id=1, source_target_pairs={{0,4},{1,5},{2,6},{3,7},{8,12},{9,13},{10,14},{11,15},{16,20},{17,... | collective-permute-start | bytes 122888 | tf_op jit(solution)/shard_map/ppermute | solution.py:21
  644.6 4.6 copy-start.7
  651.9 10.2 %copy-start.5 = (f32[5]{0:T(128)S(1)}, f32[5]{0:T(128)}, u32[]{:S(2)}) copy-start(f32[5]{0:T(128)} %constant.78) | copy-start | bytes 64
  664.2 9.9 %collective-permute-start.7 = (f32[5,32,1,1024]{3,1,0,2:T(8,128)S(1)}, f32[5,32,1,1024]{3,1,0,2:T(8,128)S(1)}, u32[]{:S(2)}, u32[]{:S(2)}) collective-permute-start(f32[5,32,1,1024]{3,1,0,2:T(8,128)S(1)} %get-tuple-element.28), channel_id=1, source_target_pairs={{0,1},{1,2},{2,3},{4,5},{5,6},{6,7},{8,9},{9,10},{10,11},{12,13},{... | collective-permute-start | bytes 1966088 | tf_op jit(solution)/shard_map/ppermute | solution.py:21
  666.7 11.9 %collective-permute-start.6 = (f32[5,32,1,1024]{3,1,0,2:T(8,128)S(1)}, f32[5,32,1,1024]{3,1,0,2:T(8,128)S(1)}, u32[]{:S(2)}, u32[]{:S(2)}) collective-permute-start(f32[5,32,1,1024]{3,1,0,2:T(8,128)S(1)} %get-tuple-element.29), channel_id=1, source_target_pairs={{1,0},{2,1},{3,2},{5,4},{6,5},{7,6},{9,8},{10,9},{11,10},{13,12},{... | collective-permute-start | bytes 1966088 | tf_op jit(solution)/shard_map/ppermute | solution.py:22
  668.7 5.6 collective-permute-start.4
  670.0 5.2 collective-permute-start.5
  679.8 10.0 %collective-permute-start.11 = (f32[5,32,1,1024]{3,1,0,2:T(8,128)S(1)}, f32[5,32,1,1024]{3,1,0,2:T(8,128)S(1)}, u32[]{:S(2)}, u32[]{:S(2)}) collective-permute-start(f32[5,32,1,1024]{3,1,0,2:T(8,128)S(1)} %get-tuple-element.24), channel_id=1, source_target_pairs={{0,1},{1,2},{2,3},{4,5},{5,6},{6,7},{8,9},{9,10},{10,11},{12,13},{... | collective-permute-start | bytes 1966088 | tf_op jit(solution)/shard_map/ppermute | solution.py:21
  681.7 11.9 %collective-permute-start.10 = (f32[5,32,1,1024]{3,1,0,2:T(8,128)S(1)}, f32[5,32,1,1024]{3,1,0,2:T(8,128)S(1)}, u32[]{:S(2)}, u32[]{:S(2)}) collective-permute-start(f32[5,32,1,1024]{3,1,0,2:T(8,128)S(1)} %get-tuple-element.25), channel_id=1, source_target_pairs={{1,0},{2,1},{3,2},{5,4},{6,5},{7,6},{9,8},{10,9},{11,10},{13,12},{... | collective-permute-start | bytes 1966088 | tf_op jit(solution)/shard_map/ppermute | solution.py:22
  684.2 5.7 collective-permute-start.8
  685.5 5.2 collective-permute-start.9
  694.8 9.7 %collective-permute-start.15 = (f32[5,32,1,1024]{3,1,0,2:T(8,128)S(1)}, f32[5,32,1,1024]{3,1,0,2:T(8,128)S(1)}, u32[]{:S(2)}, u32[]{:S(2)}) collective-permute-start(f32[5,32,1,1024]{3,1,0,2:T(8,128)S(1)} %get-tuple-element.20), channel_id=1, source_target_pairs={{0,1},{1,2},{2,3},{4,5},{5,6},{6,7},{8,9},{9,10},{10,11},{12,13},{... | collective-permute-start | bytes 1966088 | tf_op jit(solution)/shard_map/ppermute | solution.py:21
  696.7 11.9 %collective-permute-start.14 = (f32[5,32,1,1024]{3,1,0,2:T(8,128)S(1)}, f32[5,32,1,1024]{3,1,0,2:T(8,128)S(1)}, u32[]{:S(2)}, u32[]{:S(2)}) collective-permute-start(f32[5,32,1,1024]{3,1,0,2:T(8,128)S(1)} %get-tuple-element.21), channel_id=1, source_target_pairs={{1,0},{2,1},{3,2},{5,4},{6,5},{7,6},{9,8},{10,9},{11,10},{13,12},{... | collective-permute-start | bytes 1966088 | tf_op jit(solution)/shard_map/ppermute | solution.py:22
  699.2 5.4 collective-permute-start.12
  700.5 5.2 collective-permute-start.13
where the time goes:
time: 722 us; the launch traced here: 716 us
  waiting for transfers between devices  252 us (35%)
  local copies, waits for them, and re-layouts  225 us (31%)
  matrix products  143 us (20%)
  starting transfers between devices  51.5 us (7%)
  other arithmetic  34.3 us (5%)
  blocking collectives  8.99 us (1%)
    all_to_all x1, waiting for transfers between devices, on_device(): lax.all_to_all(stacked, 'az', split_axis=1, concat_axis=2, tiled=True)  137 us
    unnamed x20, local copies, waits for them, and re-layouts  112 us
    all_to_all x1, waiting for transfers between devices, on_device(): lax.all_to_all(moved, 'az', split_axis=2, concat_axis=1, tiled=True)  102 us
    all_to_all x3, local copies, waits for them, and re-layouts, on_device(): lax.all_to_all(moved, 'az', split_axis=2, concat_axis=1, tiled=True)  32.1 us
    another operation x2, local copies, waits for them, and re-layouts, on_device(): spectral_shift(piece.reshape(-1, piece.shape[2]), shift_value)  28.5 us
    ppermute x8, starting transfers between devices, padded(): before = lax.ppermute(last, axis, up)  26.7 us
    another operation x2, local copies, waits for them, and re-layouts, spectral_shift(): grid = rows.reshape(count, outer, inner)  21.5 us
    dot_general x1, matrix products, spectral_shift(): jnp.einsum('bkq,qm->bkm', twist_im, cos_inner, precision=hp)  19.1 us
  transfers between devices with their start and end apart: 18, of which 9 were waited for; matrix products, arithmetic and copies ran while one was open for 16% of the time, Pallas kernels for 0%

commit v1 on v0

--- a/solution.py
+++ b/solution.py
@@ -80,7 +80,9 @@
     shift_value = shift[0]
     piece = lax.all_to_all(stacked, "az", split_axis=1, concat_axis=2, tiled=True)
     moved = spectral_shift(piece.reshape(-1, piece.shape[2]), shift_value).reshape(piece.shape)
-    shifted_flat = lax.all_to_all(moved, "az", split_axis=2, concat_axis=1, tiled=True)
+    shifted_flat = jnp.concatenate(
+        lax.all_to_all(jnp.stack(jnp.split(moved, lax.axis_size("az"), axis=2)), "az", 0, 0), axis=1
+    )
     shifted_cycle = shifted_flat.reshape(layers, variables, radial, sector)
     weights = jnp.array(LAYER_WEIGHTS, jnp.float32)
     depth, count, rows, width = shifted_cycle.shape

time: 722 us -> 556 us (0.77)
  local copies, waits for them, and re-layouts: 225 us -> 73.6 us
  other arithmetic: 34.3 us -> 19 us
    unnamed x20 -> x18, local copies, waits for them, and re-layouts: 112 us -> 2.53 us
    all_to_all x3 -> x0, local copies, waits for them, and re-layouts: 32.1 us -> none  [on_device(): lax.all_to_all(moved, 'az', split_axis=2, concat_axis=1, tiled=True)]
    another operation x2 -> x1, local copies, waits for them, and re-layouts: 28.5 us -> 9.73 us  [on_device(): spectral_shift(piece.reshape(-1, piece.shape[2]), shift_value)]
    all_to_all x1 -> x0, other arithmetic: 18.3 us -> none  [on_device(): lax.all_to_all(moved, 'az', split_axis=2, concat_axis=1, tiled=True)]
  transfers between devices with their start and end apart: 18 -> 18, of which waited for: 9 -> 10; matrix products, arithmetic and copies ran while one was open for 16% -> 3% of each run, Pallas kernels for 0% -> 0%
where the time goes in v1:
time: 556 us; the launch traced here: 551 us
  waiting for transfers between devices  254 us (46%)
  matrix products  143 us (26%)
  local copies, waits for them, and re-layouts  73.6 us (13%)
  starting transfers between devices  50.4 us (9%)
  other arithmetic  19 us (3%)
  blocking collectives  9.05 us (2%)
    all_to_all x1, waiting for transfers between devices, on_device(): lax.all_to_all(stacked, 'az', split_axis=1, concat_axis=2, tiled=True)  137 us
    all_to_all x1, waiting for transfers between devices, on_device(): lax.all_to_all(jnp.stack(jnp.split(moved, lax.axis_size('az'), axis=2)),...  101 us
    ppermute x8, starting transfers between devices, padded(): before = lax.ppermute(last, axis, up)  24.1 us
    another operation x2, local copies, waits for them, and re-layouts, spectral_shift(): grid = rows.reshape(count, outer, inner)  21.4 us
    dot_general x1, matrix products, spectral_shift(): jnp.einsum('bkq,qm->bkm', twist_im, cos_inner, precision=hp)  19.1 us
    ppermute x8, starting transfers between devices, padded(): after = lax.ppermute(leading, axis, down)  15.2 us
    dot_general x1, matrix products, spectral_shift(): jnp.einsum('bkm,qm->bkq', mixed_im, cos_inner, precision=hp)  15 us
    dot_general x1, matrix products, spectral_shift(): jnp.einsum('bkq,qm->bkm', twist_re, sin_inner, precision=hp)  13.8 us
  transfers between devices with their start and end apart: 18, of which 10 were waited for; matrix products, arithmetic and copies ran while one was open for 3% of the time, Pallas kernels for 0%

profile of v1, /device:TPU:1, one launch (start us, length us, event | category | flops | bytes accessed | tf_op | source)
XLA Modules:
  0.0 551.3 jit_solution(4089097650420636597)
XLA Ops:
  0.6 8.2 %copy.151 = f32[20,64,1024]{2,0,1:T(8,128)} copy(f32[20,64,1024]{2,1,0:T(8,128)} %bitcast.99) | data formatting | bytes 10485760 | tf_op jit(solution)/shard_map/reshape | solution.py:79
  8.8 6.0 %all-to-all-start = ((f32[20,64,1024]{2,0,1:T(8,128)}), f32[20,64,1024]{2,0,1:T(8,128)}, u32[]{:S(2)}, u32[]{:S(2)}) async-start(f32[20,64,1024]{2,0,1:T(8,128)} %copy.151), calls=%async_computation | async-start | bytes 12582912 | tf_op jit(solution)/shard_map/all_to_all | solution.py:81
  15.9 137.3 %all-to-all-done = f32[20,64,1024]{2,0,1:T(8,128)} async-done(((f32[20,64,1024]{2,0,1:T(8,128)}), f32[20,64,1024]{2,0,1:T(8,128)}, u32[]{:S(2)}, u32[]{:S(2)}) %all-to-all-start) | async-done | bytes 5242912 | tf_op jit(solution)/shard_map/all_to_all | solution.py:81
  153.3 8.5 %copy.153 = f32[20,16,4,1024]{3,2,1,0:T(4,128)} copy(f32[20,16,4,1024]{3,0,1,2:T(8,128)} %bitcast.5) | data formatting | bytes 10485760 | tf_op jit(solution)/shard_map/all_to_all | solution.py:81
  161.8 9.6 %reshape_reshape.9 = f32[320,64,64]{2,1,0:T(8,128)} reshape(f32[20,16,4,1024]{3,2,1,0:T(4,128)} %copy.153) | data formatting | bytes 10485760 | tf_op jit(solution)/shard_map/reshape;reshape | solution.py:44
  171.4 11.8 %copy.155 = f32[320,64,64]{0,1,2:T(8,128)} copy(f32[320,64,64]{2,1,0:T(8,128)} %reshape_reshape.9) | data formatting | bytes 10485760 | tf_op jit(solution)/shard_map/reshape;reshape | solution.py:44
  183.2 8.7 %fusion.44 = f32[64,320,64]{1,0,2:T(8,128)S(1)} fusion(f32[320,64,64]{0,1,2:T(8,128)} %copy.155), kind=kOutput, calls=%fused_computation.90 | convolution fusion | flops 1006690304 | bytes 10485760 | tf_op jit(solution)/shard_map/bpq,pk->bkq/dot_general | solution.py:46
  191.9 7.6 %add_bitcast_fusion = (f32[320,64,64]{0,1,2:T(8,128)S(1)}, f32[320,64,64]{0,1,2:T(8,128)S(1)}) fusion(f32[64,320,64]{1,0,2:T(8,128)S(1)} %fusion.44, f32[64,64]{0,1:T(8,128)S(1)} %copy.159, f32[64,64]{0,1:T(8,128)S(1)} %copy.156, f32[320,64,64]{0,1,2:T(8,128)S(1)} %copy-done.2), kind=kOutput, calls=%fused_computation.10 | convolution fusion | flops 1015865344 | bytes 21004288 | tf_op jit(solution)/shard_map/bpq,pk->bkq/dot_general | solution.py:45
  199.5 13.8 %fusion.8 = f32[320,64,64]{0,2,1:T(8,128)} fusion(f32[320,64,64]{0,1,2:T(8,128)S(1)} %get-tuple-element.14), kind=kOutput, calls=%fused_computation.15 | convolution fusion | flops 1006690304 | bytes 10485760 | tf_op jit(solution)/shard_map/bkq,qm->bkm/dot_general | solution.py:52
  213.3 13.2 %fusion.10 = f32[320,64,64]{0,2,1:T(8,128)} fusion(f32[320,64,64]{0,1,2:T(8,128)S(1)} %get-tuple-element.14), kind=kOutput, calls=%fused_computation.17 | convolution fusion | flops 1006690304 | bytes 10485760 | tf_op jit(solution)/shard_map/bkq,qm->bkm/dot_general | solution.py:49
  226.5 13.6 %fusion.6 = f32[320,64,64]{0,2,1:T(8,128)} fusion(f32[320,64,64]{0,1,2:T(8,128)S(1)} %get-tuple-element.15), kind=kOutput, calls=%fused_computation.13 | convolution fusion | flops 1006690304 | bytes 10485760 | tf_op jit(solution)/shard_map/bkq,qm->bkm/dot_general | solution.py:49
  240.1 19.1 %multiply_subtract_fusion.1 = (f32[320,64,64]{0,2,1:T(8,128)}, f32[320,64,64]{0,2,1:T(8,128)S(1)}) fusion(f32[64,64]{1,0:T(8,128)S(1)} %get-tuple-element.37, f32[64,64]{1,0:T(8,128)S(1)} %get-tuple-element.36, f32[320,64,64]{0,2,1:T(8,128)} %fusion.8, f32[320,64,64]{0,2,1:T(8,128)} %fusion.10, f32[320,64,64]{0,2,1:T(8,128)} %fusion.6, ...), kind=kOutput, calls=%fused_computation.8 | convolution fusion | flops 1017176064 | bytes 31490048 | tf_op jit(solution)/shard_map/bkq,qm->bkm/dot_general | solution.py:52
  259.2 10.2 %fusion.38 = f32[320,64,64]{0,2,1:T(8,128)} fusion(f32[320,64,64]{0,2,1:T(8,128)} %get-tuple-element.12), kind=kOutput, calls=%fused_computation.84 | convolution fusion | flops 1006690304 | bytes 10485760 | tf_op jit(solution)/shard_map/bkm,qm->bkq/dot_general | solution.py:66
  269.4 7.8 %fusion.53 = f32[320,64,64]{0,2,1:T(8,128)} fusion(f32[320,64,64]{0,2,1:T(8,128)S(1)} %copy-done), kind=kOutput, calls=%fused_computation.99 | convolution fusion | flops 1006690304 | bytes 10485760 | tf_op jit(solution)/shard_map/bkm,qm->bkq/dot_general | solution.py:63
  277.3 7.9 %fusion.40 = f32[320,64,64]{0,2,1:T(8,128)} fusion(f32[320,64,64]{0,2,1:T(8,128)S(1)} %get-tuple-element.13), kind=kOutput, calls=%fused_computation.86 | convolution fusion | flops 1006690304 | bytes 10485760 | tf_op jit(solution)/shard_map/bkm,qm->bkq/dot_general | solution.py:63
  285.2 15.0 %multiply_subtract_fusion = (f32[320,64,64]{0,2,1:T(8,128)}, f32[320,64,64]{0,2,1:T(8,128)}) fusion(f32[64,64]{1,0:T(8,128)S(1)} %get-tuple-element.38, f32[64,64]{1,0:T(8,128)S(1)} %get-tuple-element.39, f32[320,64,64]{0,2,1:T(8,128)} %fusion.38, f32[320,64,64]{0,2,1:T(8,128)} %fusion.53, f32[320,64,64]{0,2,1:T(8,128)} %fusion.40, ...), kind=kOutput, calls=%fused_computation.6 | convolution fusion | flops 1017176064 | bytes 31490048 | tf_op jit(solution)/shard_map/bkm,qm->bkq/dot_general | solution.py:66
  300.1 12.4 %fusion = f32[64,320,64]{1,0,2:T(8,128)S(1)} fusion(f32[320,64,64]{0,2,1:T(8,128)} %get-tuple-element.11), kind=kOutput, calls=%fused_computation | convolution fusion | flops 1006690304 | bytes 10485760 | tf_op jit(solution)/shard_map/bkq,pk->bpq/dot_general | solution.py:71
  312.5 11.4 %multiply_bitcast_fusion = f32[320,64,64]{0,1,2:T(8,128)} fusion(f32[64,320,64]{1,0,2:T(8,128)S(1)} %fusion, f32[320,64,64]{0,2,1:T(8,128)S(1)} %copy-done.3), kind=kOutput, calls=%fused_computation.4 | convolution fusion | flops 1009311744 | bytes 15728640 | tf_op jit(solution)/shard_map/bkq,pk->bpq/dot_general | solution.py:71
  324.0 12.5 %copy.170 = f32[320,64,64]{2,1,0:T(8,128)} copy(f32[320,64,64]{0,1,2:T(8,128)} %multiply_bitcast_fusion) | data formatting | bytes 10485760 | tf_op jit(solution)/shard_map/div | solution.py:74
  336.5 9.7 %reshape_reshape.10 = f32[20,16,4096]{2,1,0:T(8,128)} reshape(f32[320,64,64]{2,1,0:T(8,128)} %copy.170) | data formatting | bytes 10485760 | tf_op jit(solution)/shard_map/reshape;reshape | solution.py:82
  346.3 3.1 slice_bitcast_fusion.3
  352.5 5.2 all-to-all-start.1
  359.1 4.0 collective-permute-start.1
  364.5 3.7 collective-permute-start.2
  368.2 3.3 collective-permute-start.3
  371.5 101.3 %all-to-all-done.1 = f32[4,20,16,1024]{3,2,1,0:T(8,128)} async-done(((f32[4,20,16,1024]{3,2,1,0:T(8,128)}), f32[4,20,16,1024]{3,2,1,0:T(8,128)}, u32[]{:S(2)}, u32[]{:S(2)}) %all-to-all-start.1) | async-done | bytes 5242912 | tf_op jit(solution)/shard_map/all_to_all | solution.py:84
  472.8 5.7 %copy.171 = f32[20,4,16,1024]{3,2,1,0:T(8,128)} copy(f32[20,4,16,1024]{3,2,0,1:T(8,128)} %bitcast.20) | data formatting | bytes 10485760 | tf_op jit(solution)/shard_map/reshape | solution.py:83
  478.5 4.6 reduce_sum.9
  485.9 9.0 %all_gather.3 = f32[5,32,1024]{2,1,0:T(8,128)S(1)} all-gather(f32[5,8,1024]{2,1,0:T(8,128)S(1)} %bitcast_multiply_fusion), channel_id=1, replica_groups=mesh['az'=4,'rad'=2,'ax'=4] {'ax'}, dimensions={1}, use_global_device_ids=true | all-gather | bytes 819200 | tf_op jit(solution)/shard_map/all_gather | solution.py:90
  502.7 3.1 collective-permute-start.5
  535.5 4.0 collective-permute-start.13
  543.5 5.5 multiply_add_fusion.2
  (71 shorter events, 52.4 us)
Async XLA Ops:
  8.8 144.4 %all-to-all-start = ((f32[20,64,1024]{2,0,1:T(8,128)}), f32[20,64,1024]{2,0,1:T(8,128)}, u32[]{:S(2)}, u32[]{:S(2)}) async-start(f32[20,64,1024]{2,0,1:T(8,128)} %copy.151), calls=%async_computation | async-start | bytes 12582912 | tf_op jit(solution)/shard_map/all_to_all | solution.py:81
  183.2 8.7 %copy-start.2 = (f32[320,64,64]{0,1,2:T(8,128)S(1)}, f32[320,64,64]{0,1,2:T(8,128)}, u32[]{:S(2)}) copy-start(f32[320,64,64]{0,1,2:T(8,128)} %copy.155) | copy-start | bytes 15728644
  199.5 27.0 %copy-start.1 = (f32[320,64,64]{0,1,2:T(8,128)}, f32[320,64,64]{0,1,2:T(8,128)S(1)}, u32[]{:S(2)}) copy-start(f32[320,64,64]{0,1,2:T(8,128)S(1)} %get-tuple-element.15) | copy-start | bytes 15728644
  259.2 10.2 %copy-start = (f32[320,64,64]{0,2,1:T(8,128)S(1)}, f32[320,64,64]{0,2,1:T(8,128)}, u32[]{:S(2)}) copy-start(f32[320,64,64]{0,2,1:T(8,128)} %get-tuple-element.12) | copy-start | bytes 15728644
  300.1 12.4 %copy-start.3 = (f32[320,64,64]{0,2,1:T(8,128)S(1)}, f32[320,64,64]{0,2,1:T(8,128)}, u32[]{:S(2)}) copy-start(f32[320,64,64]{0,2,1:T(8,128)} %get-tuple-element.10) | copy-start | bytes 15728644
  352.5 5.2 copy-start.4
  352.5 120.4 %all-to-all-start.1 = ((f32[4,20,16,1024]{3,2,1,0:T(8,128)}), f32[4,20,16,1024]{3,2,1,0:T(8,128)}, u32[]{:S(2)}, u32[]{:S(2)}) async-start(f32[4,20,16,1024]{3,2,1,0:T(8,128)} %pad_maximum_fusion), calls=%async_computation.1 | async-start | bytes 10485760 | tf_op jit(solution)/shard_map/all_to_all | solution.py:84
  357.7 138.4 %collective-permute-start = (f32[5,1,2,1024]{3,1,0,2:T(1,128)S(1)}, f32[5,1,2,1024]{3,1,0,2:T(1,128)S(1)}, u32[]{:S(2)}, u32[]{:S(2)}) collective-permute-start(f32[5,1,2,1024]{3,1,0,2:T(1,128)S(1)} %copy.145), channel_id=1, source_target_pairs={{4,0},{5,1},{6,2},{7,3},{12,8},{13,9},{14,10},{15,11},{20,16},{21,... | collective-permute-start | bytes 122888 | tf_op jit(solution)/shard_map/ppermute | solution.py:22
  359.1 137.0 %collective-permute-start.1 = (f32[5,1,2,1024]{3,1,0,2:T(1,128)S(1)}, f32[5,1,2,1024]{3,1,0,2:T(1,128)S(1)}, u32[]{:S(2)}, u32[]{:S(2)}) collective-permute-start(f32[5,1,2,1024]{3,1,0,2:T(1,128)S(1)} %copy.147), channel_id=1, source_target_pairs={{0,4},{1,5},{2,6},{3,7},{8,12},{9,13},{10,14},{11,15},{16,20},{17,... | collective-permute-start | bytes 122888 | tf_op jit(solution)/shard_map/ppermute | solution.py:21
  363.5 8.0 %copy-start.6 = (s32[32,2]{0,1:T(2,128)S(1)}, s32[32,2]{0,1:T(2,128)}, u32[]{:S(2)}) copy-start(s32[32,2]{0,1:T(2,128)} %param.9) | copy-start | bytes 772
  364.5 131.6 %collective-permute-start.2 = (f32[5,32,1,1024]{3,1,0,2:T(8,128)S(1)}, f32[5,32,1,1024]{3,1,0,2:T(8,128)}, u32[]{:S(2)}, u32[]{:S(2)}) collective-permute-start(f32[5,32,1,1024]{3,1,0,2:T(8,128)S(1)} %get-tuple-element.33), channel_id=1, source_target_pairs={{1,0},{2,1},{3,2},{5,4},{6,5},{7,6},{9,8},{10,9},{11,10},{13,12},{... | collective-permute-start | bytes 1966088 | tf_op jit(solution)/shard_map/ppermute | solution.py:22
  368.2 126.7 %collective-permute-start.3 = (f32[5,32,1,1024]{3,1,0,2:T(8,128)}, f32[5,32,1,1024]{3,1,0,2:T(8,128)}, u32[]{:S(2)}, u32[]{:S(2)}) collective-permute-start(f32[5,32,1,1024]{3,1,0,2:T(8,128)} %get-tuple-element.32), channel_id=1, source_target_pairs={{0,1},{1,2},{2,3},{4,5},{5,6},{6,7},{8,9},{9,10},{10,11},{12,13},{... | collective-permute-start | bytes 1966088 | tf_op jit(solution)/shard_map/ppermute | solution.py:21
  478.5 4.6 copy-start.7
  485.8 10.3 %copy-start.5 = (f32[5]{0:T(128)S(1)}, f32[5]{0:T(128)}, u32[]{:S(2)}) copy-start(f32[5]{0:T(128)} %constant.78) | copy-start | bytes 64
  498.3 9.9 %collective-permute-start.7 = (f32[5,32,1,1024]{3,1,0,2:T(8,128)S(1)}, f32[5,32,1,1024]{3,1,0,2:T(8,128)S(1)}, u32[]{:S(2)}, u32[]{:S(2)}) collective-permute-start(f32[5,32,1,1024]{3,1,0,2:T(8,128)S(1)} %get-tuple-element.30), channel_id=1, source_target_pairs={{0,1},{1,2},{2,3},{4,5},{5,6},{6,7},{8,9},{9,10},{10,11},{12,13},{... | collective-permute-start | bytes 1966088 | tf_op jit(solution)/shard_map/ppermute | solution.py:21
  500.6 11.9 %collective-permute-start.6 = (f32[5,32,1,1024]{3,1,0,2:T(8,128)S(1)}, f32[5,32,1,1024]{3,1,0,2:T(8,128)S(1)}, u32[]{:S(2)}, u32[]{:S(2)}) collective-permute-start(f32[5,32,1,1024]{3,1,0,2:T(8,128)S(1)} %get-tuple-element.31), channel_id=1, source_target_pairs={{1,0},{2,1},{3,2},{5,4},{6,5},{7,6},{9,8},{10,9},{11,10},{13,12},{... | collective-permute-start | bytes 1966088 | tf_op jit(solution)/shard_map/ppermute | solution.py:22
  502.7 5.5 %collective-permute-start.5 = (f32[5,1,2,1024]{3,1,0,2:T(1,128)S(1)}, f32[5,1,2,1024]{3,1,0,2:T(1,128)S(1)}, u32[]{:S(2)}, u32[]{:S(2)}) collective-permute-start(f32[5,1,2,1024]{3,1,0,2:T(1,128)S(1)} %get-tuple-element.29), channel_id=1, source_target_pairs={{0,4},{1,5},{2,6},{3,7},{8,12},{9,13},{10,14},{11,15},{16,20},{17,... | collective-permute-start | bytes 122888 | tf_op jit(solution)/shard_map/ppermute | solution.py:21
  505.8 5.4 collective-permute-start.4
  513.7 10.4 %collective-permute-start.11 = (f32[5,32,1,1024]{3,1,0,2:T(8,128)S(1)}, f32[5,32,1,1024]{3,1,0,2:T(8,128)S(1)}, u32[]{:S(2)}, u32[]{:S(2)}) collective-permute-start(f32[5,32,1,1024]{3,1,0,2:T(8,128)S(1)} %get-tuple-element.26), channel_id=1, source_target_pairs={{0,1},{1,2},{2,3},{4,5},{5,6},{6,7},{8,9},{9,10},{10,11},{12,13},{... | collective-permute-start | bytes 1966088 | tf_op jit(solution)/shard_map/ppermute | solution.py:21
  516.6 11.9 %collective-permute-start.10 = (f32[5,32,1,1024]{3,1,0,2:T(8,128)S(1)}, f32[5,32,1,1024]{3,1,0,2:T(8,128)S(1)}, u32[]{:S(2)}, u32[]{:S(2)}) collective-permute-start(f32[5,32,1,1024]{3,1,0,2:T(8,128)S(1)} %get-tuple-element.27), channel_id=1, source_target_pairs={{1,0},{2,1},{3,2},{5,4},{6,5},{7,6},{9,8},{10,9},{11,10},{13,12},{... | collective-permute-start | bytes 1966088 | tf_op jit(solution)/shard_map/ppermute | solution.py:22
  518.6 5.6 %collective-permute-start.9 = (f32[5,1,2,1024]{3,1,0,2:T(1,128)S(1)}, f32[5,1,2,1024]{3,1,0,2:T(1,128)S(1)}, u32[]{:S(2)}, u32[]{:S(2)}) collective-permute-start(f32[5,1,2,1024]{3,1,0,2:T(1,128)S(1)} %get-tuple-element.25), channel_id=1, source_target_pairs={{0,4},{1,5},{2,6},{3,7},{8,12},{9,13},{10,14},{11,15},{16,20},{17,... | collective-permute-start | bytes 122888 | tf_op jit(solution)/shard_map/ppermute | solution.py:21
  521.1 5.4 collective-permute-start.8
  529.7 9.7 %collective-permute-start.15 = (f32[5,32,1,1024]{3,1,0,2:T(8,128)S(1)}, f32[5,32,1,1024]{3,1,0,2:T(8,128)S(1)}, u32[]{:S(2)}, u32[]{:S(2)}) collective-permute-start(f32[5,32,1,1024]{3,1,0,2:T(8,128)S(1)} %get-tuple-element.22), channel_id=1, source_target_pairs={{0,1},{1,2},{2,3},{4,5},{5,6},{6,7},{8,9},{9,10},{10,11},{12,13},{... | collective-permute-start | bytes 1966088 | tf_op jit(solution)/shard_map/ppermute | solution.py:21
  531.6 11.9 %collective-permute-start.14 = (f32[5,32,1,1024]{3,1,0,2:T(8,128)S(1)}, f32[5,32,1,1024]{3,1,0,2:T(8,128)S(1)}, u32[]{:S(2)}, u32[]{:S(2)}) collective-permute-start(f32[5,32,1,1024]{3,1,0,2:T(8,128)S(1)} %get-tuple-element.23), channel_id=1, source_target_pairs={{1,0},{2,1},{3,2},{5,4},{6,5},{7,6},{9,8},{10,9},{11,10},{13,12},{... | collective-permute-start | bytes 1966088 | tf_op jit(solution)/shard_map/ppermute | solution.py:22
  534.2 5.4 collective-permute-start.12
  535.5 5.2 collective-permute-start.13
